TPU v7x, 256 devices: a whole 4x4x8 slice. The times are simulated.
256 devices in a mesh: ex: 32 (over z, y_lo, core), tok: 8 (over y_hi, x).
Axes of the slice: x: 4, y: 4 (y_hi: 2, y_lo: 2; y = y_hi * 2 + y_lo), z: 8, core: 2. Of those that a mesh axis runs over, the one named last changes fastest.
Arguments:
- activations: bfloat16 [8192, 32, 4096], P(('ex', 'tok')), may hold values from -6 to 6
- out_grads: bfloat16 [8192, 32, 2, 1024], P(('ex', 'tok')), may hold values from -6 to 6
- block_len: int32 [8192], P(('ex', 'tok')), may hold values from 1 to 32
- block_dest: int32 [8192, 1], P(('ex', 'tok')), may hold values from 0 to 31; in each aligned block of 32 rows (0 to 31, 32 to 63, ...) at most 2 rows name the same one
- block_slot: int32 [8192], P(('ex', 'tok')), may hold values from 0 to 3
- in_proj: bfloat16 [4096, 128], replicated, may hold values from -0.09375 to 0.09375
- out_proj: bfloat16 [2, 1024, 64], replicated, may hold values from -0.1875 to 0.1875
- query_grads: float32 [64, 8192], P('ex'), may hold values from -6 to 6
- precond: float32 [2, 2, 64, 64], replicated, may hold values from -2 to 2, as said below
Outputs:
- scores: float32 [64, 128], P('tok', 'ex')
Inputs may be any that keep to these rules, and one draw needn't show every extreme that they name: `block_dest`: among the 32 blocks of one device no index of ex is named more than 2 times, a bound that some device reaches; every index of ex is named by some block of the whole array. `precond`: entries of order one or less.
All inputs are finite; a program needn't handle non-finite values.
Results may differ from a plain program's by a relative error of at most 0.0003.
Values sent between devices are 32-bit elements; how exact they have to be, the bound alone decides.
A program may use at most 64 MiB of HBM per device.

v0:
```python
import jax
import jax.numpy as jnp
from jax import lax
from jax.sharding import PartitionSpec as P

R = 64
BLK = 32
EX_DEV = 4
F = 8192
highest = lax.Precision.HIGHEST


def on_device(
    activations,
    out_grads,
    block_len,
    block_dest,
    block_slot,
    in_proj,
    out_proj,
    query_grads,
    precond,
):
    block_count = activations.shape[0]
    block_size = activations.shape[1]
    ex_count = lax.axis_size("ex")
    proj_in = jnp.dot(
        activations.reshape(block_count * block_size, -1),
        in_proj,
        preferred_element_type=jnp.float32,
    )
    proj_in = proj_in.reshape(block_count, block_size, 2, R)
    proj_out = jnp.einsum("btlk,lkr->btlr", out_grads, out_proj, preferred_element_type=jnp.float32)
    position = lax.broadcasted_iota(jnp.int32, (block_count, block_size), 1)
    live_mask = (position < block_len[:, None]).astype(jnp.float32)
    proj_out = proj_out * live_mask[:, :, None, None]
    partial_value = jnp.einsum("btlo,btli->bloi", proj_out, proj_in, precision=highest).reshape(
        block_count, F
    )
    target = block_dest[:, 0]
    example = target * EX_DEV + block_slot
    by_example = (
        example[:, None] == jnp.arange(ex_count * EX_DEV, dtype=jnp.int32)[None, :]
    ).astype(jnp.float32)
    table = jnp.dot(by_example.T, partial_value, precision=highest)
    features = lax.psum_scatter(table, "ex", scatter_dimension=0, tiled=True)
    query_count = query_grads.shape[0]
    queries = query_grads.reshape(query_count, 2, R, R)
    left_side = jnp.einsum("lab,qlbc->qlac", precond[:, 0], queries, precision=highest)
    conditioned = jnp.einsum("qlac,lcd->qlad", left_side, precond[:, 1], precision=highest).reshape(
        query_count, F
    )
    score_terms = jnp.dot(
        lax.all_gather(conditioned, "ex", axis=0, tiled=True), features.T, precision=highest
    ) * (1.0 / (R * BLK))
    return lax.psum_scatter(score_terms, "tok", scatter_dimension=0, tiled=True)


def solution(mesh):
    placed = (
        P(("ex", "tok"), None, None),
        P(("ex", "tok"), None, None, None),
        P(("ex", "tok")),
        P(("ex", "tok"), None),
        P(("ex", "tok")),
        P(),
        P(),
        P("ex", None),
        P(),
    )
    return jax.shard_map(
        on_device, mesh=mesh, in_specs=placed, out_specs=P("tok", "ex"), check_vma=False
    )
```

profile of v0, /device:TPU:0, one launch (start us, length us, event | category | flops | bytes accessed | tf_op | source)
XLA Modules:
  0.0 353.2 jit_solution(176973868079033243)
XLA Ops:
  6.5 0.0 copy-start
  6.5 0.0 all-gather.3.cloned.1.call-start
  6.5 1.0 reshape.37
  7.6 1.2 convolution_bitcast_fusion.1
  8.8 1.2 convolution_bitcast_fusion
  10.0 0.7 reshape.40
  10.8 0.0 all-gather.3.cloned.1.call-update
  10.8 0.0 all-reduce.4.cloned.1.call-start
  10.9 1.5 copy.20
  12.3 0.7 fusion.18
  13.1 0.0 copy-done
  13.1 3.4 fusion.7
  16.5 4.9 %fusion = f32[32,32,2,64]{3,1,2,0:T(8,128)S(1)} fusion(bf16[2,64,4096,1]{2,1,0,3:T(8,128)(2,1)S(1)} %bitcast.51, bf16[32,32,4096]{2,1,0:T(8,128)(2,1)} %param.9), kind=kOutput, calls=%fused_computation | convolution fusion | flops 1073741824 | bytes 9961472 | tf_op jit(solution)/shard_map/dot_general | solution.py:27
  21.4 0.0 copy-start.1
  21.4 0.0 copy-start.2
  21.4 3.7 %fusion.21 = f32[32,2,64,64]{3,2,1,0:T(8,128)S(1)} fusion(f32[32,32,2,64]{3,1,2,0:T(8,128)S(1)} %fusion.7, f32[32,32,2,64]{3,1,2,0:T(8,128)S(1)} %fusion), kind=kOutput, calls=%fused_computation.24 | convolution fusion | flops 100663296 | bytes 2097152 | tf_op jit(solution)/shard_map/btlo,btli->bloi/dot_general | solution.py:37
  25.2 0.7 reshape.39
  25.8 0.0 copy-done.1
  25.8 0.0 copy-done.2
  25.9 0.0 copy-start.4
  25.9 0.0 copy-start.3
  25.9 3.9 %fusion.17 = f32[128,8192]{1,0:T(8,128)} fusion(f32[32,8192]{1,0:T(8,128)S(1)} %reshape.39, s32[32]{0:T(128)S(1)} %bitcast_add_fusion), kind=kOutput, calls=%fused_computation.18 | convolution fusion | flops 402657280 | bytes 5243008 | tf_op jit(solution)/shard_map/dot_general | solution.py:45
  29.8 0.0 all-reduce.4.cloned.1.call-update
  29.8 0.0 copy-done.4
  29.8 0.6 dynamic-slice
  30.4 0.0 copy-done.3
  30.4 0.6 dynamic-slice.2
  32.2 44.6 %all-gather.3.cloned.1.call-done = f32[32,2,8192]{2,1,0:T(2,128)} async-done(((f32[1,2,8192]{2,1,0:T(2,128)}), f32[32,2,8192]{2,1,0:T(2,128)}) %all-gather.3.cloned.1.call-update) | async-done | bytes 2097168 | tf_op jit(solution)/shard_map/all_gather | solution.py:54
  76.7 2.7 reshape.41
  79.4 239.2 %all-reduce.4.cloned.1.call-done = f32[128,8192]{1,0:T(8,128)} async-done(((f32[128,8192]{1,0:T(8,128)}), f32[128,8192]{1,0:T(8,128)}) %all-reduce.4.cloned.1.call-update) | async-done | bytes 4194320
  318.6 2.7 convolution_multiply_fusion
  321.3 24.5 %all-reduce.1 = f32[64,4]{0,1:T(4,128)S(1)} all-reduce(f32[64,4]{0,1:T(4,128)S(1)} %convolution_multiply_fusion), channel_id=3, replica_groups=mesh['ex'=32,'tok'=8] {'tok'}, use_global_device_ids=true, to_apply=%region_1.0.clone | all-reduce | flops 256 | bytes 2048
  345.7 0.7 constant_dynamic-slice_fusion
  (2 shorter events, 0.0 us)
Async XLA Ops:
  6.5 6.5 %copy-start = (bf16[2,1024,64]{1,2,0:T(8,128)(2,1)S(1)}, bf16[2,1024,64]{1,2,0:T(8,128)(2,1)}, u32[]{:S(2)}) copy-start(bf16[2,1024,64]{1,2,0:T(8,128)(2,1)} %param.15) | copy-start | bytes 786436
  6.5 70.2 %all-gather.3.cloned.1.call-start = ((), (), s32[]{:S(2)}) async-start(), calls=%async_computation | async-start | bytes 2162688 | tf_op jit(solution)/shard_map/all_gather | solution.py:54
  10.8 307.8 %all-reduce.4.cloned.1.call-start = ((), (), s32[]{:S(2)}) async-start(), calls=%async_computation.1 | async-start | bytes 8388608
  21.4 4.4 %copy-start.1 = (s32[32]{0:T(128)S(1)}, s32[32]{0:T(128)}, u32[]{:S(2)}) copy-start(s32[32]{0:T(128)} %param.13) | copy-start | bytes 388
  21.4 4.4 %copy-start.2 = (s32[32,1]{0,1:T(1,128)S(1)}, s32[32,1]{0,1:T(1,128)}, u32[]{:S(2)}) copy-start(s32[32,1]{0,1:T(1,128)} %param.12) | copy-start | bytes 388
  25.9 3.9 %copy-start.4 = (u32[256]{0:T(256)S(1)}, u32[256]{0:T(256)}, u32[]{:S(2)}) copy-start(u32[256]{0:T(256)} %constant.12) | copy-start | bytes 3076
  25.9 4.5 %copy-start.3 = (u32[256]{0:T(256)S(1)}, u32[256]{0:T(256)}, u32[]{:S(2)}) copy-start(u32[256]{0:T(256)} %constant.16) | copy-start | bytes 3076
Sparse Core Ops, SparseCore 0:
  10.9 65.7 all-gather.2
  79.4 239.1 all-reduce.3
where the time goes:
time: 354 us; the launch traced here: 353 us
  waiting for transfers between devices  284 us (80%)
  blocking collectives  24.5 us (7%)
  matrix products  21.1 us (6%)
  between operations  14.7 us (4%)
  local copies, waits for them, and re-layouts  8.42 us (2%)
    unnamed x3, waiting for transfers between devices  239 us
    all_gather x1, waiting for transfers between devices, on_device(): lax.all_gather(conditioned, 'ex', axis=0, tiled=True)  44.6 us
    unnamed x1, blocking collectives  24.5 us
  transfers between devices with their start and end apart: 2, of which 2 were waited for; matrix products, arithmetic and copies ran while one was open for 6% of the time, Pallas kernels for 0%

commit v1 on v0

--- a/solution.py
+++ b/solution.py
@@ -51,7 +51,11 @@
         query_count, F
     )
     score_terms = jnp.dot(
-        lax.all_gather(conditioned, "ex", axis=0, tiled=True), features.T, precision=highest
+        jnp.concatenate(
+            lax.all_to_all(jnp.stack([conditioned] * lax.axis_size("ex")), "ex", 0, 0), axis=0
+        ),
+        features.T,
+        precision=highest,
     ) * (1.0 / (R * BLK))
     return lax.psum_scatter(score_terms, "tok", scatter_dimension=0, tiled=True)
 

time: 354 us -> 316 us (0.89)
  waiting for transfers between devices: 284 us -> 240 us
  starting transfers between devices: 0.04 us -> 8.35 us
    all_to_all x0 -> x1, waiting for transfers between devices: none -> 50 us  [on_device(): lax.all_to_all(jnp.stack([conditioned] * lax.axis_size('ex')), 'ex', 0, 0)]
    unnamed x3 -> x2, waiting for transfers between devices: 239 us -> 190 us
    all_gather x1 -> x0, waiting for transfers between devices: 44.6 us -> none  [on_device(): lax.all_gather(conditioned, 'ex', axis=0, tiled=True)]
    all_to_all x0 -> x1, starting transfers between devices: none -> 8.35 us  [on_device(): lax.all_to_all(jnp.stack([conditioned] * lax.axis_size('ex')), 'ex', 0, 0)]
  transfers between devices with their start and end apart: 2 -> 2, of which waited for: 2 -> 2; matrix products, arithmetic and copies ran while one was open for 6% -> 2% of each run, Pallas kernels for 0% -> 0%
where the time goes in v1:
time: 316 us
  waiting for transfers between devices  240 us (76%)
  blocking collectives  24.5 us (8%)
  matrix products  18 us (6%)
  between operations  14.9 us (5%)
  local copies, waits for them, and re-layouts  9.09 us (3%)
  starting transfers between devices  8.35 us (3%)
    unnamed x2, waiting for transfers between devices  190 us
    all_to_all x1, waiting for transfers between devices, on_device(): lax.all_to_all(jnp.stack([conditioned] * lax.axis_size('ex')), 'ex', 0, 0)  50 us
    unnamed x1, blocking collectives  24.5 us
    all_to_all x1, starting transfers between devices, on_device(): lax.all_to_all(jnp.stack([conditioned] * lax.axis_size('ex')), 'ex', 0, 0)  8.35 us
  transfers between devices with their start and end apart: 2, of which 2 were waited for; matrix products, arithmetic and copies ran while one was open for 2% of the time, Pallas kernels for 0%

profile of v1, /device:TPU:0, one launch (start us, length us, event | category | flops | bytes accessed | tf_op | source)
XLA Modules:
  0.0 315.6 jit_solution(13139260914456991955)
XLA Ops:
  6.5 0.0 copy-start
  6.5 0.0 all-reduce.4.cloned.1.call-start
  6.5 1.5 copy.20
  8.1 0.7 fusion.18
  8.8 0.0 copy-start.3
  8.8 5.0 %fusion = f32[32,32,2,64]{3,1,2,0:T(8,128)S(1)} fusion(bf16[2,64,4096,1]{2,1,0,3:T(8,128)(2,1)S(1)} %bitcast.51, bf16[32,32,4096]{2,1,0:T(8,128)(2,1)} %param.9), kind=kOutput, calls=%fused_computation | convolution fusion | flops 1073741824 | bytes 9961472 | tf_op jit(solution)/shard_map/dot_general | solution.py:27
  13.8 0.0 copy-done
  13.8 0.0 copy-done.3
  13.8 1.2 fusion.7
  15.1 0.0 copy-start.4
  15.1 0.0 copy-start.5
  15.1 3.7 %fusion.21 = f32[32,2,64,64]{3,2,1,0:T(8,128)S(1)} fusion(f32[32,32,2,64]{3,1,2,0:T(8,128)S(1)} %fusion.7, f32[32,32,2,64]{3,1,2,0:T(8,128)S(1)} %fusion), kind=kOutput, calls=%fused_computation.24 | convolution fusion | flops 100663296 | bytes 2097152 | tf_op jit(solution)/shard_map/btlo,btli->bloi/dot_general | solution.py:37
  18.9 0.7 reshape.41
  19.5 0.0 copy-done.4
  19.5 0.0 copy-done.5
  19.5 0.0 copy-start.2
  19.6 0.0 copy-start.1
  19.6 3.9 %fusion.17 = f32[128,8192]{1,0:T(8,128)} fusion(f32[32,8192]{1,0:T(8,128)S(1)} %reshape.41, s32[32]{0:T(128)S(1)} %bitcast_add_fusion), kind=kOutput, calls=%fused_computation.18 | convolution fusion | flops 402657280 | bytes 5243008 | tf_op jit(solution)/shard_map/dot_general | solution.py:45
  23.5 0.0 all-reduce.4.cloned.1.call-update
  23.5 0.0 copy-done.2
  23.5 0.0 copy-start.7
  23.5 0.0 copy-start.6
  23.5 0.1 reshape.39
  23.7 0.0 copy-done.1
  23.7 0.4 convolution_bitcast_fusion.1
  24.1 0.4 convolution_bitcast_fusion
  24.5 0.1 stack_reshape.2
  24.6 2.3 stack.3
  26.9 8.3 %all-to-all-start = ((f32[32,2,8192]{2,1,0:T(2,128)}), f32[32,2,8192]{2,1,0:T(2,128)S(1)}, u32[]{:S(2)}, u32[]{:S(2)}) async-start(f32[32,2,8192]{2,1,0:T(2,128)} %stack.3), calls=%async_computation | async-start | bytes 4194304 | tf_op jit(solution)/shard_map/all_to_all | solution.py:55
  35.2 0.0 copy-done.7
  35.2 0.6 dynamic-slice
  35.8 0.0 copy-done.6
  35.8 0.7 dynamic-slice.2
  37.8 50.0 %all-to-all-done = f32[32,2,8192]{2,1,0:T(2,128)S(1)} async-done(((f32[32,2,8192]{2,1,0:T(2,128)}), f32[32,2,8192]{2,1,0:T(2,128)S(1)}, u32[]{:S(2)}, u32[]{:S(2)}) %all-to-all-start) | async-done | bytes 2097184 | tf_op jit(solution)/shard_map/all_to_all | solution.py:55
  87.8 2.4 reshape.40
  90.2 190.1 %all-reduce.4.cloned.1.call-done = f32[128,8192]{1,0:T(8,128)} async-done(((f32[128,8192]{1,0:T(8,128)}), f32[128,8192]{1,0:T(8,128)}) %all-reduce.4.cloned.1.call-update) | async-done | bytes 4194320
  280.4 3.3 %convolution_multiply_fusion = f32[64,4]{0,1:T(4,128)S(1)} fusion(f32[64,8192]{1,0:T(8,128)} %reshape.40, f32[128,8192]{1,0:T(8,128)} %all-reduce.4.cloned.1.call-done, u32[]{:T(128)S(6)} %multiply.1), kind=kOutput, calls=%fused_computation.8 | convolution fusion | flops 25166080 | bytes 2229252 | tf_op jit(solution)/shard_map/dot_general | solution.py:53
  283.7 24.5 %all-reduce.1 = f32[64,4]{0,1:T(4,128)S(1)} all-reduce(f32[64,4]{0,1:T(4,128)S(1)} %convolution_multiply_fusion), channel_id=3, replica_groups=mesh['ex'=32,'tok'=8] {'tok'}, use_global_device_ids=true, to_apply=%region_1.0.clone | all-reduce | flops 256 | bytes 2048
  308.1 0.7 constant_dynamic-slice_fusion
  (2 shorter events, 0.0 us)
Async XLA Ops:
  6.5 7.3 %copy-start = (bf16[2,1024,64]{1,2,0:T(8,128)(2,1)S(1)}, bf16[2,1024,64]{1,2,0:T(8,128)(2,1)}, u32[]{:S(2)}) copy-start(bf16[2,1024,64]{1,2,0:T(8,128)(2,1)} %param.15) | copy-start | bytes 786436
  6.5 273.8 %all-reduce.4.cloned.1.call-start = ((), (), s32[]{:S(2)}) async-start(), calls=%async_computation.1 | async-start | bytes 8388608
  8.8 5.0 %copy-start.3 = (bf16[32,32,2,1024]{3,2,1,0:T(2,128)(2,1)S(1)}, bf16[32,32,2,1024]{3,2,1,0:T(2,128)(2,1)}, u32[]{:S(2)}) copy-start(bf16[32,32,2,1024]{3,2,1,0:T(2,128)(2,1)} %param.10) | copy-start | bytes 12582916
  15.1 4.4 %copy-start.4 = (s32[32]{0:T(128)S(1)}, s32[32]{0:T(128)}, u32[]{:S(2)}) copy-start(s32[32]{0:T(128)} %param.13) | copy-start | bytes 388
  15.1 4.4 %copy-start.5 = (s32[32,1]{0,1:T(1,128)S(1)}, s32[32,1]{0,1:T(1,128)}, u32[]{:S(2)}) copy-start(s32[32,1]{0,1:T(1,128)} %param.12) | copy-start | bytes 388
  19.5 3.9 %copy-start.2 = (f32[2,8192]{1,0:T(2,128)S(1)}, f32[2,8192]{1,0:T(2,128)}, u32[]{:S(2)}) copy-start(f32[2,8192]{1,0:T(2,128)} %param.16) | copy-start | bytes 196612
  19.6 4.1 %copy-start.1 = (f32[2,2,64,64]{3,2,1,0:T(8,128)S(1)}, f32[2,2,64,64]{3,2,1,0:T(8,128)}, u32[]{:S(2)}) copy-start(f32[2,2,64,64]{3,2,1,0:T(8,128)} %param.17) | copy-start | bytes 196612
  23.5 11.7 %copy-start.7 = (u32[256]{0:T(256)S(1)}, u32[256]{0:T(256)}, u32[]{:S(2)}) copy-start(u32[256]{0:T(256)} %constant.12) | copy-start | bytes 3076
  23.5 12.3 %copy-start.6 = (u32[256]{0:T(256)S(1)}, u32[256]{0:T(256)}, u32[]{:S(2)}) copy-start(u32[256]{0:T(256)} %constant.16) | copy-start | bytes 3076
  26.9 60.9 %all-to-all-start = ((f32[32,2,8192]{2,1,0:T(2,128)}), f32[32,2,8192]{2,1,0:T(2,128)S(1)}, u32[]{:S(2)}, u32[]{:S(2)}) async-start(f32[32,2,8192]{2,1,0:T(2,128)} %stack.3), calls=%async_computation | async-start | bytes 4194304 | tf_op jit(solution)/shard_map/all_to_all | solution.py:55
Sparse Core Ops, SparseCore 0:
  23.6 256.7 all-reduce.3
